TPU v7x, 512 devices: a whole 4x4x16 slice. The times are simulated.
512 devices in a mesh: pipe: 8 (over y, core), ctx: 32 (over x, z_lo), tp: 2 (over z_hi).
Axes of the slice: x: 4, y: 4, z: 16 (z_hi: 2, z_lo: 8; z = z_hi * 8 + z_lo), core: 2. Of those that a mesh axis runs over, the one named last changes fastest.
Arguments:
- stream: bfloat16 [8, 4096, 4096], P('pipe', 'ctx', 'tp'), may hold values from -6 to 6
- queries: bfloat16 [8, 4096, 4096], P('pipe', 'ctx', 'tp'), may hold values from -5 to 5
- keys: bfloat16 [8, 4096, 1024], P('pipe', 'ctx', 'tp'), may hold values from -5 to 5
- values: bfloat16 [8, 4096, 1024], P('pipe', 'ctx', 'tp'), may hold values from -6 to 6
- segments: int32 [8, 4096], P('pipe', 'ctx'), may hold values from 0 to 5, never falling along the last dimension, each value on 1 to 2048 neighbouring positions
- norm_gain: bfloat16 [4096], P('tp'), may hold values from 0.25 to 1.75
Outputs:
- arrived: bfloat16 [8, 4096, 4096], P('pipe', 'ctx', 'tp')
- normed: bfloat16 [8, 4096, 4096], P('pipe', 'ctx', 'tp')
Inputs may be any that keep to these rules, and one draw needn't show every extreme that they name: `segments`: in each section's micro-batch the document number never falls along positions; each document holds 1 to half of 4096 positions, and one holds exactly half of 4096.
All inputs are finite; a program needn't handle non-finite values.
Results may differ from a plain program's by a relative error of at most 0.006.
Values may be sent and summed in bfloat16 or wider, within the bound.
A program may use at most 128 MiB of HBM per device.

v0:
```python
import jax
import jax.numpy as jnp
from jax import lax
from jax.sharding import PartitionSpec as P

QUERY_HEADS = 32
HEAD_SIZE = 128


def from_behind(block, axis, distance):
    devices = range(lax.axis_size(axis))
    route = [((i - distance) % len(devices), i) for i in devices]
    return lax.ppermute(block, axis, route)


def per_device(stream, queries, keys, values, segments, norm_gain):
    row_count = stream.shape[1]
    kv_width = keys.shape[2]
    kv_heads = kv_width // HEAD_SIZE
    query_group_size = queries.shape[2] // kv_width
    score_scale = HEAD_SIZE ** (-0.5)
    ctx_index = lax.axis_index("ctx")
    query_head_stack = (
        queries[0]
        .reshape(row_count, kv_heads, query_group_size, HEAD_SIZE)
        .transpose(1, 2, 0, 3)
        .reshape(kv_heads, query_group_size * row_count, HEAD_SIZE)
    )
    own_pos = ctx_index * row_count + jnp.arange(row_count, dtype=jnp.int32)
    query_pos = jnp.tile(own_pos, query_group_size)
    query_seg = jnp.tile(segments[0], query_group_size)
    query_row_block = query_group_size * row_count
    key_piece = lax.all_gather(keys[0], "ctx", axis=0, tiled=True)
    running_max = jnp.full((kv_heads, query_row_block), -1e30, jnp.float32)
    key_count = key_piece.shape[0]
    key_head_stack = key_piece.reshape(key_count, kv_heads, HEAD_SIZE)
    value_head_stack = lax.all_gather(values[0], "ctx", axis=0, tiled=True).reshape(
        key_count, kv_heads, HEAD_SIZE
    )
    scores = (
        jnp.einsum(
            "hrd,khd->hrk", query_head_stack, key_head_stack, preferred_element_type=jnp.float32
        )
        * score_scale
    )
    key_pos = jnp.arange(key_count, dtype=jnp.int32)
    allowed = (
        (key_pos[None, :] <= query_pos[:, None])
        & (lax.all_gather(segments[0], "ctx", axis=0, tiled=True)[None, :] == query_seg[:, None])
        & jnp.bool_(True)
    )
    scores = jnp.where(allowed[None], scores, -1e30)
    new_max = jnp.maximum(running_max, jnp.max(scores, axis=-1))
    weights = jnp.where(allowed[None], jnp.exp(scores - new_max[..., None]), 0.0)
    new_sum = jnp.sum(weights, axis=-1)
    new_acc = jnp.einsum(
        "hrk,khd->hrd",
        weights.astype(jnp.bfloat16),
        value_head_stack,
        preferred_element_type=jnp.float32,
    )
    final_state = (new_max, new_sum, new_acc)
    running_max, running_sum, running_acc = final_state
    mixed = (running_acc / running_sum[..., None]).astype(jnp.bfloat16)
    attended = (
        mixed.reshape(kv_heads, query_group_size, row_count, HEAD_SIZE)
        .transpose(2, 0, 1, 3)
        .reshape(row_count, kv_width * query_group_size)
    )
    attended = lax.optimization_barrier(attended).astype(jnp.float32)
    advanced = (stream[0].astype(jnp.float32) + attended).astype(jnp.bfloat16)
    arrived = from_behind(advanced[None], "pipe", 1)
    wide = arrived.astype(jnp.float32)
    squares = jnp.sum(wide * wide, axis=-1)
    totals = lax.psum(squares, "tp")
    inverse = lax.rsqrt(totals / (QUERY_HEADS * HEAD_SIZE) + 1e-05)
    normed = (wide * inverse[..., None] * norm_gain.astype(jnp.float32)).astype(jnp.bfloat16)
    return (arrived, normed)


def solution(mesh):
    in_specs = (
        P("pipe", "ctx", "tp"),
        P("pipe", "ctx", "tp"),
        P("pipe", "ctx", "tp"),
        P("pipe", "ctx", "tp"),
        P("pipe", "ctx"),
        P("tp"),
    )
    out_specs = (P("pipe", "ctx", "tp"), P("pipe", "ctx", "tp"))
    return jax.shard_map(
        per_device, mesh=mesh, in_specs=in_specs, out_specs=out_specs, check_vma=False
    )
```

profile of v0, /device:TPU:8, one launch (start us, length us, event | category | flops | bytes accessed | tf_op | source)
XLA Modules:
  0.0 487.5 jit_solution(13736906237650311648)
XLA Ops:
  7.2 0.0 all-gather.6.cloned.1.call-start
  7.2 1.7 copy.11
  8.9 0.0 all-gather.6.cloned.1.call-update
  8.9 0.0 all-gather.8.cloned.1.call-start
  8.9 1.7 copy.13
  10.6 0.0 all-gather.8.cloned.1.call-update
  10.6 1.4 reshape_squeeze.3
  12.0 0.1 copy.10
  12.2 125.1 %all-gather = s32[1,4096]{1,0:T(1,128)S(1)} all-gather(s32[1,128]{1,0:T(1,128)} %param.10), channel_id=2, replica_groups=mesh['pipe'=8,'ctx'=32,'tp'=2] {'ctx'}, dimensions={1}, use_global_device_ids=true | all-gather | bytes 16896 | tf_op jit(solution)/shard_map/all_gather | solution.py:49
  137.3 0.7 broadcast_bitcast_fusion
  138.0 2.2 fusion.6
  140.2 88.0 %all-gather.6.cloned.1.call-done = bf16[1,4096,512]{1,2,0:T(8,128)(2,1)} async-done(((bf16[1,128,512]{1,2,0:T(8,128)(2,1)}), bf16[1,4096,512]{1,2,0:T(8,128)(2,1)}) %all-gather.6.cloned.1.call-update) | async-done | bytes 4194320 | tf_op jit(solution)/shard_map/all_gather | solution.py:33
  228.2 16.7 %fusion = (f32[4,512]{1,0:T(4,128)S(1)}, f32[4,512,4096]{2,1,0:T(8,128)}) fusion(pred[512,4096]{1,0:T(8,128)(4,1)S(1)} %fusion.6, bf16[4,512,128]{2,1,0:T(8,128)(2,1)S(1)} %bitcast.25, bf16[4096,4,128]{0,2,1:T(8,128)(2,1)} %bitcast.24), kind=kOutput, calls=%fused_computation.2 | convolution fusion | flops 2172647424 | bytes 40378368 | tf_op jit(solution)/shard_map/hrd,khd->hrk/dot_general | solution.py:41
  244.9 15.6 %fusion.1 = f32[4,512]{1,0:T(4,128)S(1)} fusion(f32[4,512,4096]{2,1,0:T(8,128)} %get-tuple-element.3, f32[4,512]{1,0:T(4,128)S(1)} %broadcast_maximum_fusion, pred[512,4096]{1,0:T(8,128)(4,1)S(1)} %fusion.6), kind=kLoop, calls=%fused_computation.3 | loop fusion | flops 41940992 | bytes 35667968 | tf_op jit(solution)/shard_map/reduce_sum | solution.py:55
  260.5 178.8 %all-gather.8.cloned.1.call-done = bf16[1,4096,512]{1,2,0:T(8,128)(2,1)} async-done(((bf16[1,128,512]{1,2,0:T(8,128)(2,1)}), bf16[1,4096,512]{1,2,0:T(8,128)(2,1)}) %all-gather.8.cloned.1.call-update) | async-done | bytes 4194320 | tf_op jit(solution)/shard_map/all_gather | solution.py:37
  439.3 0.0 copy-start
  439.3 0.0 copy-start.1
  439.3 16.1 %divide_convert_fusion = bf16[4,512,128]{2,1,0:T(8,128)(2,1)S(1)} fusion(bf16[4096,4,128]{0,2,1:T(8,128)(2,1)} %bitcast.31, f32[4,512,4096]{2,1,0:T(8,128)} %get-tuple-element.3, f32[4,512]{1,0:T(4,128)S(1)} %broadcast_maximum_fusion, pred[512,4096]{1,0:T(8,128)(4,1)S(1)} %fusion.6, f32[4,512]{1,0:T(4,128)S(1)} %fusion.1), kind=kOutput, calls=%fused_computation.16 | convolution fusion | flops 2189950976 | bytes 40386560 | tf_op jit(solution)/shard_map/hrk,khd->hrd/dot_general | solution.py:56
  455.4 0.4 copy.15
  455.8 0.4 reshape.92
  456.2 0.0 copy-done
  456.2 0.1 fusion.13
  456.4 0.0 collective-permute-start
  456.4 0.0 copy-done.1
  456.4 8.6 %collective-permute-done = bf16[1,128,2048]{2,1,0:T(8,128)(2,1)S(1)} collective-permute-done((bf16[1,128,2048]{2,1,0:T(8,128)(2,1)S(1)}, bf16[1,128,2048]{2,1,0:T(8,128)(2,1)S(1)}, u32[]{:S(2)}, u32[]{:S(2)}) %collective-permute-start) | collective-permute-done | bytes 524320 | tf_op jit(solution)/shard_map/ppermute | solution.py:13
  465.0 0.2 fusion.7
  465.2 13.6 %psum.7 = f32[1,128]{1,0:T(1,128)S(1)} all-reduce(f32[1,128]{1,0:T(1,128)S(1)} %bitcast.30), channel_id=1, replica_groups=mesh['pipe'=8,'ctx'=32,'tp'=2] {'tp'}, use_global_device_ids=true, to_apply=%region_3.4 | all-reduce | flops 128 | bytes 1024 | tf_op jit(solution)/shard_map/psum | solution.py:75
  478.8 1.0 fusion.9
  479.8 0.8 copy.19
  (4 shorter events, 0.0 us)
Async XLA Ops:
  7.2 221.0 %all-gather.6.cloned.1.call-start = ((), (), s32[]{:S(2)}) async-start(), calls=%async_computation | async-start | bytes 4325376 | tf_op jit(solution)/shard_map/all_gather | solution.py:33
  8.9 430.4 %all-gather.8.cloned.1.call-start = ((), (), s32[]{:S(2)}) async-start(), calls=%async_computation.1 | async-start | bytes 4325376 | tf_op jit(solution)/shard_map/all_gather | solution.py:37
  439.3 17.0 %copy-start = (bf16[1,128,2048]{2,1,0:T(8,128)(2,1)S(1)}, bf16[1,128,2048]{2,1,0:T(8,128)(2,1)}, u32[]{:S(2)}) copy-start(bf16[1,128,2048]{2,1,0:T(8,128)(2,1)} %param.6) | copy-start | bytes 1572868
  439.3 17.1 %copy-start.1 = (bf16[2048]{0:T(1024)(128)(2,1)S(1)}, bf16[2048]{0:T(1024)(128)(2,1)}, u32[]{:S(2)}) copy-start(bf16[2048]{0:T(1024)(128)(2,1)} %param.11) | copy-start | bytes 12292
  456.4 8.6 %collective-permute-start = (bf16[1,128,2048]{2,1,0:T(8,128)(2,1)S(1)}, bf16[1,128,2048]{2,1,0:T(8,128)(2,1)S(1)}, u32[]{:S(2)}, u32[]{:S(2)}) collective-permute-start(bf16[1,128,2048]{2,1,0:T(8,128)(2,1)S(1)} %fusion.13), channel_id=1, source_target_pairs={{448,0},{0,64},{64,128},{128,192},{192,256},{256,320},{320,384},{3... | collective-permute-start | bytes 1572872 | tf_op jit(solution)/shard_map/ppermute | solution.py:13
Sparse Core Ops, SparseCore 0:
  10.6 217.5 all-gather.5
  230.8 208.4 all-gather.7
where the time goes:
time: 488 us; the launch traced here: 487 us
  waiting for transfers between devices  275 us (56%)
  blocking collectives  139 us (28%)
  matrix products  32.8 us (7%)
  other arithmetic  19.2 us (4%)
  between operations  14.1 us (3%)
  local copies, waits for them, and re-layouts  7.12 us (1%)
    all_gather x1, waiting for transfers between devices, per_device(): lax.all_gather(values[0], 'ctx', axis=0, tiled=True)  179 us
    all_gather x1, blocking collectives, per_device(): lax.all_gather(segments[0], 'ctx', axis=0, tiled=True)[None, :]  125 us
    all_gather x1, waiting for transfers between devices, per_device(): key_piece = lax.all_gather(keys[0], 'ctx', axis=0, tiled=True)  88 us
    dot_general x1, matrix products, per_device(): jnp.einsum('hrd,khd->hrk', query_head_stack, key_head_stack, preferred_el...  16.7 us
    dot_general x1, matrix products, per_device(): jnp.einsum('hrk,khd->hrd', weights.astype(jnp.bfloat16), value_head_stack...  16.1 us
    reduce_sum x1, other arithmetic, per_device(): new_sum = jnp.sum(weights, axis=-1)  15.6 us
    psum x1, blocking collectives, per_device(): totals = lax.psum(squares, 'tp')  13.6 us
  transfers between devices with their start and end apart: 3, of which 3 were waited for; matrix products, arithmetic and copies ran while one was open for 8% of the time, Pallas kernels for 0%

commit v1 on v0

--- a/solution.py
+++ b/solution.py
@@ -5,6 +5,15 @@
 
 QUERY_HEADS = 32
 HEAD_SIZE = 128
+
+
+def edit_islands_on_mesh(point):
+    return jnp.concatenate(
+        jax.lax.all_to_all(
+            jnp.stack([point for _ in range(jax.lax.axis_size("ctx"))], axis=0), "ctx", 0, 0
+        ),
+        axis=0,
+    )
 
 
 def from_behind(block, axis, distance):
@@ -46,7 +55,7 @@
     key_pos = jnp.arange(key_count, dtype=jnp.int32)
     allowed = (
         (key_pos[None, :] <= query_pos[:, None])
-        & (lax.all_gather(segments[0], "ctx", axis=0, tiled=True)[None, :] == query_seg[:, None])
+        & (edit_islands_on_mesh(segments[0])[None, :] == query_seg[:, None])
         & jnp.bool_(True)
     )
     scores = jnp.where(allowed[None], scores, -1e30)

time: 488 us -> 487 us (level)
  blocking collectives: 139 us -> 13.6 us
  waiting for transfers between devices: 275 us -> 383 us
  starting transfers between devices: 0.1 us -> 15.5 us
    all_gather x1 -> x0, blocking collectives: 125 us -> none  [per_device(): lax.all_gather(segments[0], 'ctx', axis=0, tiled=True)[None, :]]
    all_gather x1, waiting for transfers between devices: 88 us -> 186 us  [per_device(): key_piece = lax.all_gather(keys[0], 'ctx', axis=0, tiled=True)]
    all_to_all x0 -> x1, starting transfers between devices: none -> 15.4 us  [edit_islands_on_mesh(): jax.lax.all_to_all(jnp.stack([point for _ in range(jax.lax.axis_size('ctx...]
    all_to_all x0 -> x1, waiting for transfers between devices: none -> 10.3 us  [edit_islands_on_mesh(): jax.lax.all_to_all(jnp.stack([point for _ in range(jax.lax.axis_size('ctx...]
  transfers between devices with their start and end apart: 3 -> 4, of which waited for: 3 -> 4; matrix products, arithmetic and copies ran while one was open for 8% -> 8% of each run, Pallas kernels for 0% -> 0%
where the time goes in v1:
time: 487 us
  waiting for transfers between devices  383 us (79%)
  matrix products  32.8 us (7%)
  other arithmetic  19.2 us (4%)
  starting transfers between devices  15.5 us (3%)
  between operations  14.1 us (3%)
  blocking collectives  13.6 us (3%)
  local copies, waits for them, and re-layouts  8.39 us (2%)
    all_gather x1, waiting for transfers between devices, per_device(): key_piece = lax.all_gather(keys[0], 'ctx', axis=0, tiled=True)  186 us
    all_gather x1, waiting for transfers between devices, per_device(): lax.all_gather(values[0], 'ctx', axis=0, tiled=True)  178 us
    dot_general x1, matrix products, per_device(): jnp.einsum('hrd,khd->hrk', query_head_stack, key_head_stack, preferred_el...  16.7 us
    dot_general x1, matrix products, per_device(): jnp.einsum('hrk,khd->hrd', weights.astype(jnp.bfloat16), value_head_stack...  16.1 us
    reduce_sum x1, other arithmetic, per_device(): new_sum = jnp.sum(weights, axis=-1)  15.6 us
    all_to_all x1, starting transfers between devices, edit_islands_on_mesh(): jax.lax.all_to_all(jnp.stack([point for _ in range(jax.lax.axis_size('ctx...  15.4 us
    psum x1, blocking collectives, per_device(): totals = lax.psum(squares, 'tp')  13.6 us
    all_to_all x1, waiting for transfers between devices, edit_islands_on_mesh(): jax.lax.all_to_all(jnp.stack([point for _ in range(jax.lax.axis_size('ctx...  10.3 us
  transfers between devices with their start and end apart: 4, of which 4 were waited for; matrix products, arithmetic and copies ran while one was open for 8% of the time, Pallas kernels for 0%

profile of v1, /device:TPU:8, one launch (start us, length us, event | category | flops | bytes accessed | tf_op | source)
XLA Modules:
  0.0 486.9 jit_solution(3049231343508701010)
XLA Ops:
  7.2 0.0 all-gather.5.cloned.1.call-start
  7.2 1.7 copy.11
  8.9 0.0 all-gather.5.cloned.1.call-update
  8.9 0.0 all-gather.7.cloned.1.call-start
  8.9 1.7 copy.13
  10.6 0.0 all-gather.7.cloned.1.call-update
  10.6 1.3 stack.3
  11.9 15.4 %all-to-all-start = ((s32[32,1,128]{2,1,0:T(1,128)}), s32[32,1,128]{2,1,0:T(1,128)S(1)}, u32[]{:S(2)}, u32[]{:S(2)}) async-start(s32[32,1,128]{2,1,0:T(1,128)} %stack.3), calls=%async_computation | async-start | bytes 32768 | tf_op jit(solution)/shard_map/all_to_all | solution.py:12
  27.3 0.7 broadcast_bitcast_fusion
  28.0 1.4 reshape_squeeze.3
  29.4 0.1 copy.10
  29.5 10.3 %all-to-all-done = s32[32,1,128]{2,1,0:T(1,128)S(1)} async-done(((s32[32,1,128]{2,1,0:T(1,128)}), s32[32,1,128]{2,1,0:T(1,128)S(1)}, u32[]{:S(2)}, u32[]{:S(2)}) %all-to-all-start) | async-done | bytes 16416 | tf_op jit(solution)/shard_map/all_to_all | solution.py:12
  39.8 2.2 fusion.6
  42.0 186.2 %all-gather.5.cloned.1.call-done = bf16[1,4096,512]{1,2,0:T(8,128)(2,1)} async-done(((bf16[1,128,512]{1,2,0:T(8,128)(2,1)}), bf16[1,4096,512]{1,2,0:T(8,128)(2,1)}) %all-gather.5.cloned.1.call-update) | async-done | bytes 4194320 | tf_op jit(solution)/shard_map/all_gather | solution.py:42
  228.2 16.7 %fusion = (f32[4,512]{1,0:T(4,128)S(1)}, f32[4,512,4096]{2,1,0:T(8,128)}) fusion(pred[512,4096]{1,0:T(8,128)(4,1)S(1)} %fusion.6, bf16[4,512,128]{2,1,0:T(8,128)(2,1)S(1)} %bitcast.25, bf16[4096,4,128]{0,2,1:T(8,128)(2,1)} %bitcast.24), kind=kOutput, calls=%fused_computation.2 | convolution fusion | flops 2172647424 | bytes 40378368 | tf_op jit(solution)/shard_map/hrd,khd->hrk/dot_general | solution.py:50
  244.9 15.6 %fusion.1 = f32[4,512]{1,0:T(4,128)S(1)} fusion(f32[4,512,4096]{2,1,0:T(8,128)} %get-tuple-element.3, f32[4,512]{1,0:T(4,128)S(1)} %broadcast_maximum_fusion, pred[512,4096]{1,0:T(8,128)(4,1)S(1)} %fusion.6), kind=kLoop, calls=%fused_computation.3 | loop fusion | flops 41940992 | bytes 35667968 | tf_op jit(solution)/shard_map/reduce_sum | solution.py:64
  260.5 178.2 %all-gather.7.cloned.1.call-done = bf16[1,4096,512]{1,2,0:T(8,128)(2,1)} async-done(((bf16[1,128,512]{1,2,0:T(8,128)(2,1)}), bf16[1,4096,512]{1,2,0:T(8,128)(2,1)}) %all-gather.7.cloned.1.call-update) | async-done | bytes 4194320 | tf_op jit(solution)/shard_map/all_gather | solution.py:46
  438.8 0.0 copy-start
  438.8 0.0 copy-start.1
  438.8 16.1 %divide_convert_fusion = bf16[4,512,128]{2,1,0:T(8,128)(2,1)S(1)} fusion(bf16[4096,4,128]{0,2,1:T(8,128)(2,1)} %bitcast.32, f32[4,512,4096]{2,1,0:T(8,128)} %get-tuple-element.3, f32[4,512]{1,0:T(4,128)S(1)} %broadcast_maximum_fusion, pred[512,4096]{1,0:T(8,128)(4,1)S(1)} %fusion.6, f32[4,512]{1,0:T(4,128)S(1)} %fusion.1), kind=kOutput, calls=%fused_computation.16 | convolution fusion | flops 2189950976 | bytes 40386560 | tf_op jit(solution)/shard_map/hrk,khd->hrd/dot_general | solution.py:65
  454.9 0.4 copy.15
  455.3 0.4 reshape.103
  455.7 0.0 copy-done
  455.7 0.1 fusion.13
  455.8 0.0 collective-permute-start
  455.9 0.0 copy-done.1
  455.9 8.6 %collective-permute-done = bf16[1,128,2048]{2,1,0:T(8,128)(2,1)S(1)} collective-permute-done((bf16[1,128,2048]{2,1,0:T(8,128)(2,1)S(1)}, bf16[1,128,2048]{2,1,0:T(8,128)(2,1)S(1)}, u32[]{:S(2)}, u32[]{:S(2)}) %collective-permute-start) | collective-permute-done | bytes 524320 | tf_op jit(solution)/shard_map/ppermute | solution.py:22
  464.5 0.2 fusion.7
  464.6 13.6 %psum.7 = f32[1,128]{1,0:T(1,128)S(1)} all-reduce(f32[1,128]{1,0:T(1,128)S(1)} %bitcast.31), channel_id=1, replica_groups=mesh['pipe'=8,'ctx'=32,'tp'=2] {'tp'}, use_global_device_ids=true, to_apply=%region_3.4 | all-reduce | flops 128 | bytes 1024 | tf_op jit(solution)/shard_map/psum | solution.py:84
  478.3 1.0 fusion.9
  479.3 0.8 copy.19
  (4 shorter events, 0.0 us)
Async XLA Ops:
  7.2 221.1 %all-gather.5.cloned.1.call-start = ((), (), s32[]{:S(2)}) async-start(), calls=%async_computation.1 | async-start | bytes 4325376 | tf_op jit(solution)/shard_map/all_gather | solution.py:42
  8.9 429.9 %all-gather.7.cloned.1.call-start = ((), (), s32[]{:S(2)}) async-start(), calls=%async_computation.2 | async-start | bytes 4325376 | tf_op jit(solution)/shard_map/all_gather | solution.py:46
  11.9 27.9 %all-to-all-start = ((s32[32,1,128]{2,1,0:T(1,128)}), s32[32,1,128]{2,1,0:T(1,128)S(1)}, u32[]{:S(2)}, u32[]{:S(2)}) async-start(s32[32,1,128]{2,1,0:T(1,128)} %stack.3), calls=%async_computation | async-start | bytes 32768 | tf_op jit(solution)/shard_map/all_to_all | solution.py:12
  438.8 16.9 %copy-start = (bf16[1,128,2048]{2,1,0:T(8,128)(2,1)S(1)}, bf16[1,128,2048]{2,1,0:T(8,128)(2,1)}, u32[]{:S(2)}) copy-start(bf16[1,128,2048]{2,1,0:T(8,128)(2,1)} %param.6) | copy-start | bytes 1572868
  438.8 17.1 %copy-start.1 = (bf16[2048]{0:T(1024)(128)(2,1)S(1)}, bf16[2048]{0:T(1024)(128)(2,1)}, u32[]{:S(2)}) copy-start(bf16[2048]{0:T(1024)(128)(2,1)} %param.11) | copy-start | bytes 12292
  455.8 8.6 %collective-permute-start = (bf16[1,128,2048]{2,1,0:T(8,128)(2,1)S(1)}, bf16[1,128,2048]{2,1,0:T(8,128)(2,1)S(1)}, u32[]{:S(2)}, u32[]{:S(2)}) collective-permute-start(bf16[1,128,2048]{2,1,0:T(8,128)(2,1)S(1)} %fusion.13), channel_id=1, source_target_pairs={{448,0},{0,64},{64,128},{128,192},{192,256},{256,320},{320,384},{3... | collective-permute-start | bytes 1572872 | tf_op jit(solution)/shard_map/ppermute | solution.py:22
Sparse Core Ops, SparseCore 0:
  10.6 217.6 all-gather.4
  230.8 207.8 all-gather.6
